TPU v7x, 256 devices: a whole 4x4x8 slice. The times are simulated.
256 devices in a mesh: env: 4 (over x_lo, core), tm: 64 (over x_hi, z, y).
Axes of the slice: x: 4 (x_hi: 2, x_lo: 2; x = x_hi * 2 + x_lo), y: 4, z: 8, core: 2. Of those that a mesh axis runs over, the one named last changes fastest.
Arguments:
- hidden: bfloat16 [4, 64, 256, 1024], P('env', 'tm'), may hold values from -6 to 6
- done_step: int32 [4, 64], P('env', 'tm'), may hold values from 0 to 255
- alive: int32 [4, 64, 256], P('env', None, 'tm'), may hold values 0 or 1
- targets: float32 [4, 64, 256], P('env', None, 'tm'), may hold values from -6 to 6
- gain_t: float32 [1024], replicated, may hold values from 0.25 to 1.75
- w_qkv_t: bfloat16 [1024, 3072], replicated, may hold values from -5 to 5
- w_out_t: bfloat16 [1024, 1024], replicated, may hold values from -0.1875 to 0.1875
- gain_a: float32 [1024], replicated, may hold values from 0.25 to 1.75
- w_qkv_a: bfloat16 [1024, 3072], P('tm'), may hold values from -5 to 5
- w_out_a: bfloat16 [1024, 1024], P('tm'), may hold values from -0.1875 to 0.1875
- w_value: float32 [1024], replicated, may hold values from -0.1875 to 0.1875
Outputs:
- values: float32 [4, 64, 256], P('env', None, 'tm')
- input_grad: bfloat16 [4, 64, 256, 1024], P('env', 'tm')
- qkv_grad: float32 [1024, 3072], P('tm')
- out_grad: float32 [1024, 1024], P('tm')
Inputs may be any that keep to these rules, and one draw needn't show every extreme that they name: `done_step`: the last step of an agent's first episode in the window; later steps form a new episode.
All inputs are finite; a program needn't handle non-finite values. No bound on the sum of `alive` on one device may be relied on, other than what follows from the above.
Results may differ from a plain program's by a relative error of at most 0.02.
Values may be sent and summed in bfloat16 or wider, within the bound.
A program may use at most 128 MiB of HBM per device.

v0:
```python
import math
import jax
import jax.numpy as jnp
from jax import lax
from jax.sharding import PartitionSpec as P

HEADS = 8
HI = lax.Precision.HIGHEST


def norm_scale(rows, gain):
    return rows * lax.rsqrt(jnp.mean(rows * rows, axis=-1, keepdims=True) + 1e-06) * gain


def attend(qkv, allowed, head_count):
    width = qkv.shape[-1] // 3
    size = width // head_count
    shape = qkv.shape[:-1] + (head_count, size)
    queries = qkv[..., :width].reshape(shape)
    key_rows = qkv[..., width : 2 * width].reshape(shape)
    value_rows = qkv[..., 2 * width :].reshape(shape)
    scores = jnp.einsum("qhe,khe->hqk", queries, key_rows, preferred_element_type=jnp.float32)
    scores = jnp.where(allowed[None], scores / math.sqrt(size), -1e30)
    row_max = jnp.max(scores, axis=-1, keepdims=True)
    weights = jnp.exp(scores - row_max)
    probs = (weights / jnp.sum(weights, axis=-1, keepdims=True)).astype(jnp.bfloat16)
    mixed = jnp.einsum("hqk,khe->qhe", probs, value_rows, preferred_element_type=jnp.float32)
    return mixed.reshape(qkv.shape[:-1] + (width,))


def temporal_block(rows, done, gain, w_qkv, w_out, head_count):
    length, width = rows.shape
    rows_f = rows.astype(jnp.float32)
    normed = norm_scale(rows_f, gain).astype(jnp.bfloat16)
    qkv = jnp.dot(normed, w_qkv, preferred_element_type=jnp.float32).astype(jnp.bfloat16)
    positions = jnp.arange(length, dtype=jnp.int32)
    later = positions > done
    allowed = (positions[:, None] >= positions[None, :]) & (later[:, None] == later[None, :])
    mixed = attend(qkv, allowed, head_count).astype(jnp.bfloat16)
    added = jnp.dot(mixed, w_out, preferred_element_type=jnp.float32)
    return (rows_f + added).astype(jnp.bfloat16)


def left_product(left, right):
    return lax.dot_general(
        left, right, (((0,), (0,)), ((), ())), preferred_element_type=jnp.float32
    )


def agent_step(lifted, alive_rows, target_rows, gain, w_qk, z, w_value, head_count):
    agent_count, step_count, width = lifted.shape
    size = width // head_count
    lifted_f = lifted.astype(jnp.float32)
    normed_f, norm_pull = jax.vjp(lambda rows: norm_scale(rows, gain), lifted_f)
    normed = normed_f.astype(jnp.bfloat16).reshape(-1, width)
    qk = jnp.dot(normed, w_qk, preferred_element_type=jnp.float32).astype(jnp.bfloat16)
    qk = qk.reshape(agent_count, step_count, 2, head_count, size)
    q, k = (qk[:, :, 0], qk[:, :, 1])
    s = jnp.dot(normed.astype(jnp.float32), z, precision=HI)
    s = s.reshape(agent_count, step_count, head_count).transpose(1, 2, 0)
    living = alive_rows.T == 1
    allowed = living[:, None, :] | jnp.eye(agent_count, dtype=bool)[None]
    scores = jnp.einsum("qbhe,kbhe->bhqk", q, k, preferred_element_type=jnp.float32)
    scores = jnp.where(allowed[:, None], scores / math.sqrt(size), -1e30)
    weights = jnp.exp(scores - jnp.max(scores, axis=-1, keepdims=True))
    probs = weights / jnp.sum(weights, axis=-1, keepdims=True)
    pv = jnp.sum(probs * s[:, :, None, :], axis=-1)
    predicted = jnp.sum(lifted_f * w_value, axis=-1) + jnp.sum(pv, axis=1).T
    err = 32.0 * alive_rows.astype(jnp.float32) * (predicted - target_rows)
    weighted = probs * err.T[:, None, :, None]
    t = jnp.sum(weighted, axis=2)
    ds = weighted * (s[:, :, None, :] - pv[..., None]) * (1.0 / math.sqrt(size))
    ds = ds.astype(jnp.bfloat16)
    dq = jnp.einsum("bhqk,kbhe->qbhe", ds, k, preferred_element_type=jnp.float32)
    dk = jnp.einsum("bhqk,qbhe->kbhe", ds, q, preferred_element_type=jnp.float32)
    dqk = jnp.stack([dq, dk], axis=2).astype(jnp.bfloat16).reshape(-1, 2 * width)
    t = t.transpose(2, 0, 1).reshape(-1, head_count)
    grad_normed = jnp.dot(dqk, w_qk.T, preferred_element_type=jnp.float32)
    grad_normed = grad_normed + jnp.dot(t, z.T, precision=HI)
    grad_top = err[..., None] * w_value
    grad_lifted = grad_top + norm_pull(grad_normed.reshape(agent_count, step_count, width))[0]
    return (predicted, grad_lifted.astype(jnp.bfloat16), normed, dqk, t)


def per_device(
    hidden, done_step, alive, targets, gain_t, w_qkv_t, w_out_t, gain_a, w_qkv_a, w_out_a, w_value
):
    width = hidden.shape[-1]
    size = width // HEADS
    local_rows = hidden[0, 0]
    done = done_step[0, 0]
    v = lax.all_gather(
        jnp.sum(w_out_a.astype(jnp.float32) * w_value, axis=1), "tm", axis=0, tiled=True
    )
    w_v = w_qkv_a[:, 2 * width :].astype(jnp.float32)
    z = jnp.sum((w_v * v).reshape(-1, HEADS, size), axis=-1)
    z = lax.all_gather(z, "tm", axis=0, tiled=True)
    w_qk = lax.all_gather(w_qkv_a[:, : 2 * width], "tm", axis=0, tiled=True)
    first, pull = jax.vjp(
        lambda rows: temporal_block(rows, done, gain_t, w_qkv_t, w_out_t, HEADS), local_rows
    )
    lifted = lax.all_to_all(first[None], "tm", split_axis=1, concat_axis=0, tiled=True)
    predicted, grad_lifted, normed, dqk, t = agent_step(
        lifted, alive[0], targets[0], gain_a, w_qk, z, w_value, HEADS
    )
    returned = lax.all_to_all(grad_lifted, "tm", split_axis=0, concat_axis=1, tiled=True)
    terms = left_product(normed, dqk).astype(jnp.bfloat16)
    u_terms = lax.dot_general(normed.astype(jnp.float32), t, (((0,), (0,)), ((), ())), precision=HI)
    summed = lax.psum_scatter(terms, "tm", scatter_dimension=0, tiled=True)
    qk_grad = lax.psum(summed, "env").astype(jnp.float32)
    u_mine = lax.psum(u_terms, ("env", "tm"))
    u_mine = lax.dynamic_slice_in_dim(u_mine, lax.axis_index("tm") * w_v.shape[0], w_v.shape[0], 0)
    u_wide = jnp.repeat(u_mine, size, axis=1)
    v_grad = u_wide * v
    mixed_err = lax.psum(jnp.sum(u_wide * w_v, axis=0), "tm")
    mixed_err = lax.dynamic_slice_in_dim(
        mixed_err, lax.axis_index("tm") * w_out_a.shape[0], w_out_a.shape[0], 0
    )
    out_grad = mixed_err[:, None] * w_value
    qkv_grad = jnp.concatenate([qk_grad, v_grad], axis=1)
    input_grad = pull(returned[0])[0]
    return (predicted[None], input_grad[None, None], qkv_grad, out_grad)


def solution(mesh):
    in_specs = (
        P("env", "tm", None, None),
        P("env", "tm"),
        P("env", None, "tm"),
        P("env", None, "tm"),
        P(),
        P(),
        P(),
        P(),
        P("tm", None),
        P("tm", None),
        P(),
    )
    out_specs = (P("env", None, "tm"), P("env", "tm", None, None), P("tm", None), P("tm", None))
    return jax.shard_map(
        per_device, mesh=mesh, in_specs=in_specs, out_specs=out_specs, check_vma=False
    )
```

profile of v0, /device:TPU:1, one launch (start us, length us, event | category | flops | bytes accessed | tf_op | source)
XLA Modules:
  0.0 856.8 jit_solution(7488116643575696525)
XLA Ops:
  7.2 1.6 slice.24
  11.3 4.9 convolution_convert_fusion
  18.7 2.2 copy.97
  21.0 1.6 fusion.114
  27.5 4.5 reduce.4
  32.0 2.2 reshape.279
  34.2 15.1 %all-to-all-start = ((bf16[64,2,2048]{2,1,0:T(2,128)(2,1)}), bf16[64,2,2048]{2,1,0:T(2,128)(2,1)S(1)}, u32[]{:S(2)}, u32[]{:S(2)}) async-start(bf16[64,2,2048]{2,1,0:T(2,128)(2,1)} %reshape.279), calls=%async_computation | async-start | bytes 1048576 | tf_op jit(solution)/shard_map/all_to_all | solution.py:102
  51.0 156.9 %all-reduce.3 = f32[1024]{0:T(1024)S(1)} all-reduce(f32[1024]{0:T(1024)S(1)} %dynamic-update-slice), channel_id=1, replica_groups=mesh['env'=4,'tm'=64] {'tm'}, use_global_device_ids=true, to_apply=%add.3 | all-reduce | flops 1024 | bytes 8192
  208.9 148.0 %all-gather = f32[64,16,8]{1,2,0:T(8,128)S(1)} all-gather(f32[1,16,8]{1,2,0:T(8,128)S(1)} %bitcast.169), channel_id=1, replica_groups=mesh['env'=4,'tm'=64] {'tm'}, dimensions={0}, use_global_device_ids=true | all-gather | bytes 33280 | tf_op jit(solution)/shard_map/all_gather | solution.py:97
  357.9 1.8 reshape.280
  359.7 1.6 fusion.39
  367.1 3.5 fusion.16
  371.9 3.5 multiply_reduce_fusion.2
  376.7 3.3 convolution_bitcast_fusion
  380.0 3.4 convolution_bitcast_fusion.1
  384.8 1.7 copy.78
  386.4 2.3 convert_element_type.173
  388.7 4.6 convolution_convert_fusion.1
  394.1 1.6 multiply_reduce_fusion
  395.8 3.8 fusion.115
  399.6 2.1 fusion.40
  401.8 2.6 reshape.260
  404.4 2.8 fusion.47
  407.2 4.9 all-to-all-start.1
  413.6 132.2 %psum.22 = f32[1024,8]{0,1:T(8,128)S(1)} all-reduce(f32[1024,8]{0,1:T(8,128)S(1)} %convolution_bitcast_fusion.2), channel_id=1, replica_groups=mesh['env'=4,'tm'=64] {'env','tm'}, use_global_device_ids=true, to_apply=%region_19.20 | all-reduce | flops 8192 | bytes 65536 | tf_op jit(solution)/shard_map/psum | solution.py:111
  546.8 156.0 %psum.23 = f32[1024]{0:T(1024)S(1)} all-reduce(f32[1024]{0:T(1024)S(1)} %get-tuple-element.19), channel_id=1, replica_groups=mesh['env'=4,'tm'=64] {'tm'}, use_global_device_ids=true, to_apply=%region_21.22 | all-reduce | flops 1024 | bytes 8192 | tf_op jit(solution)/shard_map/psum | solution.py:115
  704.6 2.6 convolution_convert_fusion.5
  708.5 2.3 fusion.6
  716.0 2.9 fusion.52
  718.9 45.1 %reduce-scatter.2.cloned.1.call-done = bf16[16,2048]{1,0:T(8,128)(2,1)} async-done(((bf16[1024,2048]{1,0:T(8,128)(2,1)}), bf16[16,2048]{1,0:T(8,128)(2,1)}) %reduce-scatter.2.cloned.1.call-update) | async-done | bytes 65552 | tf_op jit(solution)/shard_map/reduce_scatter | solution.py:109
  764.1 2.3 fusion.67
  766.4 82.4 %all-reduce.6.cloned.1.call-done = bf16[16,2048]{1,0:T(8,128)(2,1)} async-done(((bf16[16,2048]{1,0:T(8,128)(2,1)}), bf16[16,2048]{1,0:T(8,128)(2,1)}) %all-reduce.6.cloned.1.call-update) | async-done | bytes 65552 | tf_op jit(solution)/shard_map/psum | solution.py:110
  (139 shorter events, 34.9 us)
Async XLA Ops:
  7.2 18.2 %copy-start = (bf16[1024,1024]{1,0:T(8,128)(2,1)S(1)}, bf16[1024,1024]{1,0:T(8,128)(2,1)}, u32[]{:S(2)}) copy-start(bf16[1024,1024]{1,0:T(8,128)(2,1)} %param.17) | copy-start | bytes 6291460
  7.2 359.9 %all-gather.3.cloned.1.call-start = ((), (), s32[]{:S(2)}) async-start(), calls=%async_computation.3 | async-start | bytes 4259840 | tf_op jit(solution)/shard_map/all_gather | solution.py:98
  11.3 4.9 copy-start.28
  17.2 6.8 copy-start.9
  18.7 3.9 copy-start.11
  22.9 2.4 copy-start.16
  22.9 2.4 copy-start.7
  26.9 22.4 %copy-start.31 = (u32[256]{0:T(256)S(1)}, u32[256]{0:T(256)}, u32[]{:S(2)}) copy-start(u32[256]{0:T(256)} %constant.61) | copy-start | bytes 3076
  26.9 23.7 %copy-start.18 = (f32[1024]{0:T(1024)S(1)}, f32[1024]{0:T(1024)}, u32[]{:S(2)}) copy-start(f32[1024]{0:T(1024)} %param.21) | copy-start | bytes 12292
  27.0 23.7 %copy-start.21 = (bf16[16,1024]{1,0:T(8,128)(2,1)S(1)}, bf16[16,1024]{1,0:T(8,128)(2,1)}, u32[]{:S(2)}) copy-start(bf16[16,1024]{1,0:T(8,128)(2,1)} %param.20) | copy-start | bytes 98308
  32.0 325.1 %copy-start.27 = (s32[1,64,4]{1,2,0:T(4,128)S(1)}, s32[1,64,4]{1,2,0:T(4,128)}, u32[]{:S(2)}) copy-start(s32[1,64,4]{1,2,0:T(4,128)} %param.13) | copy-start | bytes 3076
  34.2 323.7 %all-to-all-start = ((bf16[64,2,2048]{2,1,0:T(2,128)(2,1)}), bf16[64,2,2048]{2,1,0:T(2,128)(2,1)S(1)}, u32[]{:S(2)}, u32[]{:S(2)}) async-start(bf16[64,2,2048]{2,1,0:T(2,128)(2,1)} %reshape.279), calls=%async_computation | async-start | bytes 1048576 | tf_op jit(solution)/shard_map/all_to_all | solution.py:102
  49.3 714.7 %reduce-scatter.2.cloned.1.call-start = ((), (), s32[]{:S(2)}) async-start(), calls=%async_computation.4 | async-start | bytes 4259840 | tf_op jit(solution)/shard_map/reduce_scatter | solution.py:109
  207.9 149.2 %copy-start.19 = (f32[1024]{0:T(1024)}, f32[1024]{0:T(1024)S(1)}, u32[]{:S(2)}) copy-start(f32[1024]{0:T(1024)S(1)} %all-reduce.3) | copy-start | bytes 12292
  357.9 5.6 copy-start.15
  361.3 9.4 %copy-start.23 = (f32[256]{0:T(256)}, f32[256]{0:T(256)S(1)}, u32[]{:S(2)}) copy-start(f32[256]{0:T(256)S(1)} %get-tuple-element.24) | copy-start | bytes 3076
  384.8 4.0 copy-start.24
  401.7 2.7 copy-start.5
  404.4 7.7 copy-start.17
  404.4 141.6 %copy-start.20 = (f32[1024]{0:T(1024)S(1)}, f32[1024]{0:T(1024)}, u32[]{:S(2)}) copy-start(f32[1024]{0:T(1024)} %copy-done.19) | copy-start | bytes 12292
  407.2 296.4 %all-to-all-start.1 = ((bf16[64,4,1024]{2,1,0:T(4,128)(2,1)}), bf16[64,4,1024]{2,1,0:T(4,128)(2,1)S(1)}, u32[]{:S(2)}, u32[]{:S(2)}) async-start(bf16[64,4,1024]{2,1,0:T(4,128)(2,1)} %fusion.47), calls=%async_computation.1 | async-start | bytes 1048576 | tf_op jit(solution)/shard_map/all_to_all | solution.py:106
  412.0 436.7 %all-reduce.6.cloned.1.call-start = ((), (), s32[]{:S(2)}) async-start(), calls=%async_computation.5 | async-start | bytes 131072 | tf_op jit(solution)/shard_map/psum | solution.py:110
  704.6 3.9 copy-start.10
  708.5 2.4 copy-start.2
  710.8 1.7 copy-start.12
  712.5 2.4 slice-start
  713.8 1.5 copy-start.8
  713.8 2.2 slice-start.1
  713.8 2.2 copy-start.30
  716.0 2.9 copy-start.26
  716.0 48.0 %copy-start.14 = (bf16[256,1024]{1,0:T(8,128)(2,1)S(1)}, bf16[256,1024]{1,0:T(8,128)(2,1)}, u32[]{:S(2)}) copy-start(bf16[256,1024]{1,0:T(8,128)(2,1)} %squeeze.21) | copy-start | bytes 1572868
  716.0 48.0 %copy-start.29 = (f32[256]{0:T(256)S(1)}, f32[256]{0:T(256)}, u32[]{:S(2)}) copy-start(f32[256]{0:T(256)} %copy-done.28) | copy-start | bytes 3076
  (7 other events, 6.8 us)
Sparse Core Ops, SparseCore 0:
  12.1 128.8 all-gather.2
  393.4 370.5 reduce-scatter.1
  766.8 81.8 all-reduce.5
where the time goes:
time: 858 us; the launch traced here: 857 us
  blocking collectives  593 us (69%)
  waiting for transfers between devices  128 us (15%)
  matrix products  45.3 us (5%)
  local copies, waits for them, and re-layouts  30.5 us (4%)
  other arithmetic  24.6 us (3%)
  starting transfers between devices  20.1 us (2%)
  between operations  15.7 us (2%)
    unnamed x1, blocking collectives  157 us
    psum x1, blocking collectives, per_device(): mixed_err = lax.psum(jnp.sum(u_wide * w_v, axis=0), 'tm')  156 us
    all_gather x1, blocking collectives, per_device(): z = lax.all_gather(z, 'tm', axis=0, tiled=True)  148 us
    psum x1, blocking collectives, per_device(): u_mine = lax.psum(u_terms, ('env', 'tm'))  132 us
    psum x1, waiting for transfers between devices, per_device(): qk_grad = lax.psum(summed, 'env').astype(jnp.float32)  82.4 us
    reduce_scatter x1, waiting for transfers between devices, per_device(): summed = lax.psum_scatter(terms, 'tm', scatter_dimension=0, tiled=True)  45.1 us
  transfers between devices with their start and end apart: 5, of which 2 were waited for; matrix products, arithmetic and copies ran while one was open for 8% of the time, Pallas kernels for 0%

commit v1 on v0

--- a/solution.py
+++ b/solution.py
@@ -108,7 +108,9 @@
     u_terms = lax.dot_general(normed.astype(jnp.float32), t, (((0,), (0,)), ((), ())), precision=HI)
     summed = lax.psum_scatter(terms, "tm", scatter_dimension=0, tiled=True)
     qk_grad = lax.psum(summed, "env").astype(jnp.float32)
-    u_mine = lax.psum(u_terms, ("env", "tm"))
+    u_mine = u_terms
+    for mesh_axis in ("env", "tm"):
+        u_mine = lax.psum(u_mine, mesh_axis)
     u_mine = lax.dynamic_slice_in_dim(u_mine, lax.axis_index("tm") * w_v.shape[0], w_v.shape[0], 0)
     u_wide = jnp.repeat(u_mine, size, axis=1)
     v_grad = u_wide * v

time: 858 us -> 1080 us (1.26)
  blocking collectives: 593 us -> 831 us
  waiting for transfers between devices: 128 us -> 107 us
    psum x1 -> x2, blocking collectives: 132 us -> 376 us  [per_device(): u_mine = lax.psum(u_mine, mesh_axis)]
    reduce_scatter x1, waiting for transfers between devices: 45.1 us -> 0.02 us  [per_device(): summed = lax.psum_scatter(terms, 'tm', scatter_dimension=0, tiled=True)]
    psum x1, waiting for transfers between devices: 82.4 us -> 107 us  [per_device(): qk_grad = lax.psum(summed, 'env').astype(jnp.float32)]
  transfers between devices with their start and end apart: 5 -> 5, of which waited for: 2 -> 1; matrix products, arithmetic and copies ran while one was open for 8% -> 6% of each run, Pallas kernels for 0% -> 0%
where the time goes in v1:
time: 1080 us; the launch traced here: 1070 us
  blocking collectives  831 us (77%)
  waiting for transfers between devices  107 us (10%)
  matrix products  45.3 us (4%)
  local copies, waits for them, and re-layouts  30.4 us (3%)
  other arithmetic  24.6 us (2%)
  starting transfers between devices  20.1 us (2%)
  between operations  15.7 us (1%)
    psum x2, blocking collectives, per_device(): u_mine = lax.psum(u_mine, mesh_axis)  376 us
    unnamed x1, blocking collectives  157 us
    psum x1, blocking collectives, per_device(): mixed_err = lax.psum(jnp.sum(u_wide * w_v, axis=0), 'tm')  150 us
    all_gather x1, blocking collectives, per_device(): z = lax.all_gather(z, 'tm', axis=0, tiled=True)  148 us
    psum x1, waiting for transfers between devices, per_device(): qk_grad = lax.psum(summed, 'env').astype(jnp.float32)  107 us
  transfers between devices with their start and end apart: 5, of which 1 were waited for; matrix products, arithmetic and copies ran while one was open for 6% of the time, Pallas kernels for 0%

profile of v1, /device:TPU:1, one launch (start us, length us, event | category | flops | bytes accessed | tf_op | source)
XLA Modules:
  0.0 1074.3 jit_solution(5468325328519251238)
XLA Ops:
  7.2 1.6 slice.24
  11.3 4.9 convolution_convert_fusion
  18.7 2.2 copy.97
  21.0 1.6 fusion.114
  27.5 4.5 reduce.4
  32.0 2.2 reshape.279
  34.2 15.1 %all-to-all-start = ((bf16[64,2,2048]{2,1,0:T(2,128)(2,1)}), bf16[64,2,2048]{2,1,0:T(2,128)(2,1)S(1)}, u32[]{:S(2)}, u32[]{:S(2)}) async-start(bf16[64,2,2048]{2,1,0:T(2,128)(2,1)} %reshape.279), calls=%async_computation | async-start | bytes 1048576 | tf_op jit(solution)/shard_map/all_to_all | solution.py:102
  51.0 156.9 %all-reduce.3 = f32[1024]{0:T(1024)S(1)} all-reduce(f32[1024]{0:T(1024)S(1)} %dynamic-update-slice), channel_id=1, replica_groups=mesh['env'=4,'tm'=64] {'tm'}, use_global_device_ids=true, to_apply=%add.3 | all-reduce | flops 1024 | bytes 8192
  208.9 148.0 %all-gather = f32[64,16,8]{1,2,0:T(8,128)S(1)} all-gather(f32[1,16,8]{1,2,0:T(8,128)S(1)} %bitcast.169), channel_id=1, replica_groups=mesh['env'=4,'tm'=64] {'tm'}, dimensions={0}, use_global_device_ids=true | all-gather | bytes 33280 | tf_op jit(solution)/shard_map/all_gather | solution.py:97
  357.9 1.8 reshape.280
  359.7 1.6 fusion.39
  367.1 3.5 fusion.16
  371.9 3.5 multiply_reduce_fusion.2
  376.7 3.3 convolution_bitcast_fusion
  380.0 3.4 convolution_bitcast_fusion.1
  384.8 1.7 copy.78
  386.4 2.3 convert_element_type.173
  388.7 4.6 convolution_convert_fusion.1
  394.1 1.6 multiply_reduce_fusion
  395.8 3.8 fusion.115
  399.6 2.1 fusion.40
  401.8 2.6 reshape.260
  404.4 2.8 fusion.47
  407.2 4.9 all-to-all-start.1
  413.6 66.0 %psum.29 = f32[1024,8]{0,1:T(8,128)S(1)} all-reduce(f32[1024,8]{0,1:T(8,128)S(1)} %convolution_bitcast_fusion.2), channel_id=1, replica_groups=mesh['env'=4,'tm'=64] {'env'}, use_global_device_ids=true, to_apply=%region_19.20 | all-reduce | flops 8192 | bytes 65536 | tf_op jit(solution)/shard_map/psum | solution.py:113
  479.5 310.0 %psum.30 = f32[1024,8]{0,1:T(8,128)S(1)} all-reduce(f32[1024,8]{0,1:T(8,128)S(1)} %psum.29), channel_id=1, replica_groups=mesh['env'=4,'tm'=64] {'tm'}, use_global_device_ids=true, to_apply=%region_20.21 | all-reduce | flops 8192 | bytes 65536 | tf_op jit(solution)/shard_map/psum | solution.py:113
  790.5 150.2 %psum.31 = f32[1024]{0:T(1024)S(1)} all-reduce(f32[1024]{0:T(1024)S(1)} %get-tuple-element.19), channel_id=1, replica_groups=mesh['env'=4,'tm'=64] {'tm'}, use_global_device_ids=true, to_apply=%region_22.23 | all-reduce | flops 1024 | bytes 8192 | tf_op jit(solution)/shard_map/psum | solution.py:117
  942.4 2.6 convolution_convert_fusion.5
  946.3 2.3 fusion.6
  953.8 2.9 fusion.52
  956.8 2.3 fusion.67
  959.2 107.1 %all-reduce.6.cloned.1.call-done = bf16[16,2048]{1,0:T(8,128)(2,1)} async-done(((bf16[16,2048]{1,0:T(8,128)(2,1)}), bf16[16,2048]{1,0:T(8,128)(2,1)}) %all-reduce.6.cloned.1.call-update) | async-done | bytes 65552 | tf_op jit(solution)/shard_map/psum | solution.py:110
  (140 shorter events, 34.9 us)
Async XLA Ops:
  7.2 18.2 %copy-start = (bf16[1024,1024]{1,0:T(8,128)(2,1)S(1)}, bf16[1024,1024]{1,0:T(8,128)(2,1)}, u32[]{:S(2)}) copy-start(bf16[1024,1024]{1,0:T(8,128)(2,1)} %param.17) | copy-start | bytes 6291460
  7.2 359.9 %all-gather.3.cloned.1.call-start = ((), (), s32[]{:S(2)}) async-start(), calls=%async_computation.3 | async-start | bytes 4259840 | tf_op jit(solution)/shard_map/all_gather | solution.py:98
  11.3 4.9 copy-start.28
  17.2 6.8 copy-start.9
  18.7 3.9 copy-start.11
  22.9 2.4 copy-start.16
  22.9 2.4 copy-start.7
  26.9 22.4 %copy-start.31 = (u32[256]{0:T(256)S(1)}, u32[256]{0:T(256)}, u32[]{:S(2)}) copy-start(u32[256]{0:T(256)} %constant.61) | copy-start | bytes 3076
  26.9 23.7 %copy-start.18 = (f32[1024]{0:T(1024)S(1)}, f32[1024]{0:T(1024)}, u32[]{:S(2)}) copy-start(f32[1024]{0:T(1024)} %param.21) | copy-start | bytes 12292
  27.0 23.7 %copy-start.21 = (bf16[16,1024]{1,0:T(8,128)(2,1)S(1)}, bf16[16,1024]{1,0:T(8,128)(2,1)}, u32[]{:S(2)}) copy-start(bf16[16,1024]{1,0:T(8,128)(2,1)} %param.20) | copy-start | bytes 98308
  32.0 325.1 %copy-start.27 = (s32[1,64,4]{1,2,0:T(4,128)S(1)}, s32[1,64,4]{1,2,0:T(4,128)}, u32[]{:S(2)}) copy-start(s32[1,64,4]{1,2,0:T(4,128)} %param.13) | copy-start | bytes 3076
  34.2 323.7 %all-to-all-start = ((bf16[64,2,2048]{2,1,0:T(2,128)(2,1)}), bf16[64,2,2048]{2,1,0:T(2,128)(2,1)S(1)}, u32[]{:S(2)}, u32[]{:S(2)}) async-start(bf16[64,2,2048]{2,1,0:T(2,128)(2,1)} %reshape.279), calls=%async_computation | async-start | bytes 1048576 | tf_op jit(solution)/shard_map/all_to_all | solution.py:102
  49.3 907.5 %reduce-scatter.2.cloned.1.call-start = ((), (), s32[]{:S(2)}) async-start(), calls=%async_computation.4 | async-start | bytes 4259840 | tf_op jit(solution)/shard_map/reduce_scatter | solution.py:109
  207.9 149.2 %copy-start.19 = (f32[1024]{0:T(1024)}, f32[1024]{0:T(1024)S(1)}, u32[]{:S(2)}) copy-start(f32[1024]{0:T(1024)S(1)} %all-reduce.3) | copy-start | bytes 12292
  357.9 5.6 copy-start.15
  361.3 9.4 copy-start.23
  384.8 4.0 copy-start.24
  401.7 2.7 copy-start.5
  404.4 7.7 copy-start.17
  404.4 385.3 %copy-start.20 = (f32[1024]{0:T(1024)S(1)}, f32[1024]{0:T(1024)}, u32[]{:S(2)}) copy-start(f32[1024]{0:T(1024)} %copy-done.19) | copy-start | bytes 12292
  407.2 534.3 %all-to-all-start.1 = ((bf16[64,4,1024]{2,1,0:T(4,128)(2,1)}), bf16[64,4,1024]{2,1,0:T(4,128)(2,1)S(1)}, u32[]{:S(2)}, u32[]{:S(2)}) async-start(bf16[64,4,1024]{2,1,0:T(4,128)(2,1)} %fusion.47), calls=%async_computation.1 | async-start | bytes 1048576 | tf_op jit(solution)/shard_map/all_to_all | solution.py:106
  412.0 654.2 %all-reduce.6.cloned.1.call-start = ((), (), s32[]{:S(2)}) async-start(), calls=%async_computation.5 | async-start | bytes 131072 | tf_op jit(solution)/shard_map/psum | solution.py:110
  942.4 3.9 copy-start.10
  946.3 2.4 copy-start.2
  948.7 1.7 copy-start.12
  950.4 2.4 slice-start
  951.6 1.4 copy-start.8
  951.6 2.2 slice-start.1
  951.7 2.2 copy-start.30
  953.8 2.9 copy-start.26
  953.8 3.0 copy-start.14
  953.8 3.0 copy-start.29
  (7 other events, 6.8 us)
Sparse Core Ops, SparseCore 0:
  12.1 128.8 all-gather.2
  393.4 369.1 reduce-scatter.1
  956.9 109.2 all-reduce.5
